TPU v7x, 32 devices: a whole 2x2x4 slice. The times are simulated.
32 devices in a mesh: row: 4 (over y, core), col: 8 (over z, x).
Axes of the slice: x: 2, y: 2, z: 4, core: 2. Of those that a mesh axis runs over, the one named last changes fastest.
Arguments:
- probes: float32 [32768, 256], P(('row', 'col')), may hold values from -6 to 6
- near_blocks: bfloat16 [32, 8, 1024, 1024], P(('row', 'col')), may hold values from -0.09375 to 0.09375
- near_leaves: int32 [32, 8], P(('row', 'col')), may hold values from 0 to 7, as said below
- near_count: int32 [32], P(('row', 'col')), may hold values from 1 to 8, as said below
- leaf_rank: int32 [32], P(('row', 'col')), may hold values from 128 to 256
- leaf_basis: float32 [32768, 256], P(('row', 'col')), may hold values from -0.1875 to 0.1875
- leaf_transfer: float32 [32, 256, 512], P(('row', 'col')), may hold values from -0.125 to 0.125
- leaf_links: int32 [32, 4], P(('row', 'col')), may hold values from 0 to 7, as said below
- leaf_link_blocks: float32 [32, 4, 256, 256], P(('row', 'col')), may hold values from -0.1875 to 0.1875
- parent_links: int32 [4, 2], P('row'), may hold values from 0 to 3, as said below
- parent_link_blocks: float32 [4, 2, 512, 512], P('row'), may hold values from -0.1875 to 0.1875
Outputs:
- term_one: float32 [32768, 256], P(('row', 'col'))
- term_two: float32 [32768, 256], P(('row', 'col'))
Inputs may be any that keep to these rules, and one draw needn't show every extreme that they name: `near_leaves`: slot 0 of every leaf is the leaf's own position; slots 1 to near_count - 1 are distinct other positions of the same group; later slots repeat the leaf's own position. `near_count`: some leaf has 8 live slots in every draw. `leaf_links`: each leaf's 4 coupled positions are distinct and differ from its own. `parent_links`: each parent's 2 coupled parents are distinct and differ from itself.
All inputs are finite; a program needn't handle non-finite values.
Results may differ from a plain program's by a relative error of at most 0.0034.
Values may be sent and summed in bfloat16 or wider, within the bound.
No kernel may reach another device: no remote copies, remote signals or barrier semaphores. Data moves between devices by JAX's collectives and lax.ppermute only.
A program may use at most 128 MiB of HBM per device.

v0:
```python
import jax
import jax.numpy as jnp
from jax import lax
from jax.sharding import PartitionSpec as P


def local(
    probes,
    near_blocks,
    near_leaves,
    near_count,
    leaf_rank,
    leaf_basis,
    leaf_transfer,
    leaf_links,
    leaf_link_blocks,
    parent_links,
    parent_link_blocks,
):
    highest = lax.Precision.HIGHEST
    span_col = lax.axis_size("col")
    span_row = lax.axis_size("row")
    leaf_rows = probes.shape[0]
    probe_cols = probes.shape[1]
    rank_cols = leaf_basis.shape[1]
    parent_cols = leaf_transfer.shape[2]
    rank_mask = (jnp.arange(rank_cols, dtype=jnp.int32) < leaf_rank[0]).astype(jnp.float32)[:, None]
    transfer = leaf_transfer[0]
    own_blocks = near_blocks[0]
    own_near = near_leaves[0]

    def multiply(vector):
        packed = vector.astype(jnp.bfloat16)
        empty = jnp.zeros((leaf_rows, probe_cols), jnp.float32)
        stacked = lax.all_gather(packed, "col", axis=0, tiled=True).reshape(
            span_col, leaf_rows, probe_cols
        )

        def add_slot(slot, total):
            near_block = lax.dynamic_index_in_dim(own_blocks, slot, 0, False)
            source = lax.dynamic_index_in_dim(stacked, own_near[slot], 0, False)
            return total + jnp.dot(near_block, source, preferred_element_type=jnp.float32)

        near_sum = lax.fori_loop(0, near_count[0], add_slot, empty)
        skeleton = jnp.dot(leaf_basis.T, vector, precision=highest) * rank_mask
        gathered = lax.all_gather(skeleton, "col", axis=0, tiled=True).reshape(
            span_col, rank_cols, probe_cols
        )
        linked = gathered[leaf_links[0]]
        coupled = jnp.einsum("kab,kbp->ap", leaf_link_blocks[0], linked, precision=highest)
        upward = jnp.dot(transfer.T, skeleton, precision=highest)
        portion = lax.psum_scatter(upward, "col", scatter_dimension=1, tiled=True)
        every_parent = lax.all_gather(portion, "row", axis=0, tiled=True).reshape(
            span_row, parent_cols, -1
        )
        far_portion = jnp.einsum(
            "kab,kbp->ap", parent_link_blocks[0], every_parent[parent_links[0]], precision=highest
        )
        far_parent = lax.all_gather(far_portion, "col", axis=1, tiled=True)
        combined = (coupled + jnp.dot(transfer, far_parent, precision=highest)) * rank_mask
        return jnp.dot(leaf_basis, combined, precision=highest) + near_sum

    term_one = multiply(probes)
    term_two = 2.0 * multiply(term_one) - probes
    return (term_one, term_two)


def solution(mesh):
    in_specs = (
        P(("row", "col"), None),
        P(("row", "col"), None, None, None),
        P(("row", "col"), None),
        P(("row", "col")),
        P(("row", "col")),
        P(("row", "col"), None),
        P(("row", "col"), None, None),
        P(("row", "col"), None),
        P(("row", "col"), None, None, None),
        P("row", None),
        P("row", None, None, None),
    )
    out_specs = (P(("row", "col"), None), P(("row", "col"), None))
    return jax.shard_map(local, mesh=mesh, in_specs=in_specs, out_specs=out_specs, check_vma=False)
```

profile of v0, /device:TPU:4, one launch (start us, length us, event | category | flops | bytes accessed | tf_op | source)
XLA Modules:
  0.0 513.7 jit_solution(4543359432863506335)
XLA Ops:
  8.0 3.5 convolution_multiply_fusion.1
  11.5 2.6 convolution_bitcast_fusion.3
  14.9 0.8 convert_element_type.14
  15.9 62.3 %reduce-scatter.3.cloned.1.call-done = f32[512,32]{0,1:T(8,128)} async-done(((f32[512,256]{0,1:T(8,128)}), f32[512,32]{0,1:T(8,128)}) %reduce-scatter.3.cloned.1.call-update) | async-done | bytes 65552 | tf_op jit(solution)/shard_map/reduce_scatter | solution.py:52
  78.2 6.0 %all_gather.25 = f32[2048,32]{0,1:T(8,128)S(1)} all-gather(f32[512,32]{0,1:T(8,128)} %reduce-scatter.3.cloned.1.call-done), channel_id=1, replica_groups=mesh['row'=4,'col'=8] {'row'}, dimensions={0}, use_global_device_ids=true | all-gather | bytes 327680 | tf_op jit(solution)/shard_map/all_gather | solution.py:53
  84.8 2.0 fusion.28
  86.8 32.8 %all_gather.26 = f32[512,256]{0,1:T(8,128)S(1)} all-gather(f32[512,32]{0,1:T(8,128)S(1)} %fusion.28), channel_id=1, replica_groups=mesh['row'=4,'col'=8] {'col'}, dimensions={1}, use_global_device_ids=true | all-gather | bytes 589824 | tf_op jit(solution)/shard_map/all_gather | solution.py:59
  119.6 11.7 %all-gather.5.cloned.1.call-done = f32[2048,256]{1,0:T(8,128)} async-done(((f32[256,256]{1,0:T(8,128)}), f32[2048,256]{1,0:T(8,128)}) %all-gather.5.cloned.1.call-update) | async-done | bytes 2097168 | tf_op jit(solution)/shard_map/all_gather | solution.py:46
  131.3 3.2 gather_fusion
  134.5 3.4 convolution_bitcast_fusion.5
  138.5 68.2 %all-gather.7.cloned.1.call-done = bf16[8192,256]{1,0:T(8,128)(2,1)} async-done(((bf16[1024,256]{1,0:T(8,128)(2,1)}), bf16[8192,256]{1,0:T(8,128)(2,1)}) %all-gather.7.cloned.1.call-update) | async-done | bytes 4194320 | tf_op jit(solution)/shard_map/all_gather | solution.py:35
  206.8 45.6 %while.20 = (s32[]{:T(128)}, f32[1024,256]{1,0:T(8,128)S(1)}, s32[]{:T(128)}, bf16[8,1024,1024]{2,1,0:T(8,128)(2,1)}, s32[8]{0:T(128)S(1)}, /*index=5*/bf16[8,10...) while((s32[]{:T(128)}, f32[1024,256]{1,0:T(8,128)S(1)}, s32[]{:T(128)}, ...), condition=%wide.region_2.3_spmd, body=%wide.region_1.2_spmd.sunk | while | flops 537133056 | bytes 4718773 | solution.py:44
  210.0 2.4 fusion.67
  215.6 2.4 fusion.67
  221.2 2.4 fusion.67
  226.8 2.4 fusion.67
  232.4 2.4 fusion.67
  238.1 2.4 fusion.67
  243.7 2.4 fusion.67
  249.3 2.4 fusion.67
  252.4 1.3 copy.20
  253.7 3.5 fusion.42
  257.2 1.0 convolution_multiply_fusion
  258.6 1.4 convolution_bitcast_fusion.2
  261.2 1.4 copy.25
  262.6 2.5 copy.26
  265.1 55.6 %reduce-scatter.5.cloned.1.call-done = f32[512,32]{0,1:T(8,128)} async-done(((f32[512,256]{0,1:T(8,128)}), f32[512,32]{0,1:T(8,128)}) %reduce-scatter.5.cloned.1.call-update) | async-done | bytes 65552 | tf_op jit(solution)/shard_map/reduce_scatter | solution.py:52
  320.7 6.0 %all_gather.29 = f32[2048,32]{0,1:T(8,128)S(1)} all-gather(f32[512,32]{0,1:T(8,128)} %reduce-scatter.5.cloned.1.call-done), channel_id=1, replica_groups=mesh['row'=4,'col'=8] {'row'}, dimensions={0}, use_global_device_ids=true | all-gather | bytes 327680 | tf_op jit(solution)/shard_map/all_gather | solution.py:53
  327.3 2.0 fusion.31
  329.3 32.8 %all_gather.30 = f32[512,256]{0,1:T(8,128)S(1)} all-gather(f32[512,32]{0,1:T(8,128)S(1)} %fusion.31), channel_id=1, replica_groups=mesh['row'=4,'col'=8] {'col'}, dimensions={1}, use_global_device_ids=true | all-gather | bytes 589824 | tf_op jit(solution)/shard_map/all_gather | solution.py:59
  362.1 13.3 %all-gather.9.cloned.1.call-done = f32[2048,256]{0,1:T(8,128)} async-done(((f32[256,256]{0,1:T(8,128)}), f32[2048,256]{0,1:T(8,128)}) %all-gather.9.cloned.1.call-update) | async-done | bytes 2097168 | tf_op jit(solution)/shard_map/all_gather | solution.py:46
  375.4 3.0 copy.28
  378.4 3.2 gather_fusion.2
  381.7 3.4 convolution_bitcast_fusion.4
  385.7 63.5 %all-gather.11.cloned.1.call-done = bf16[8192,256]{0,1:T(8,128)(2,1)} async-done(((bf16[1024,256]{0,1:T(8,128)(2,1)}), bf16[8192,256]{0,1:T(8,128)(2,1)}) %all-gather.11.cloned.1.call-update) | async-done | bytes 4194320 | tf_op jit(solution)/shard_map/all_gather | solution.py:35
  449.2 6.5 %copy.29 = bf16[8192,256]{1,0:T(8,128)(2,1)} copy(bf16[8192,256]{0,1:T(8,128)(2,1)} %all-gather.11.cloned.1.call-done) | data formatting | bytes 8388608 | tf_op jit(solution)/shard_map/while | solution.py:44
  455.7 45.6 %while.21 = (s32[]{:T(128)}, f32[1024,256]{1,0:T(8,128)S(1)}, s32[]{:T(128)}, bf16[8,1024,1024]{2,1,0:T(8,128)(2,1)}, s32[8]{0:T(128)S(1)}, /*index=5*/bf16[8,10...) while((s32[]{:T(128)}, f32[1024,256]{1,0:T(8,128)S(1)}, s32[]{:T(128)}, ...), condition=%wide.region_5.6_spmd, body=%wide.region_4.5_spmd.sunk | while | flops 537133056 | bytes 4718773 | solution.py:44
  458.9 2.4 fusion.70
  464.5 2.4 fusion.70
  470.2 2.4 fusion.70
  475.8 2.4 fusion.70
  481.4 2.4 fusion.70
  487.0 2.4 fusion.70
  492.6 2.4 fusion.70
  498.3 2.4 fusion.70
  501.3 1.3 copy.24
  502.6 2.9 fusion.25
  505.6 1.3 copy.27
  (67 shorter events, 14.4 us)
Async XLA Ops:
  7.2 77.6 %copy-start = (f32[1,2,512,512]{3,2,1,0:T(8,128)S(1)}, f32[1,2,512,512]{3,2,1,0:T(8,128)}, u32[]{:S(2)}) copy-start(f32[1,2,512,512]{3,2,1,0:T(8,128)} %param.25) | copy-start | bytes 6291460
  7.2 71.1 %reduce-scatter.3.cloned.1.call-start = ((), (), s32[]{:S(2)}) async-start(), calls=%async_computation.3 | async-start | bytes 589824 | tf_op jit(solution)/shard_map/reduce_scatter | solution.py:52
  8.0 6.9 %copy-start.2 = (f32[1024,256]{1,0:T(8,128)S(1)}, f32[1024,256]{1,0:T(8,128)}, u32[]{:S(2)}) copy-start(f32[1024,256]{1,0:T(8,128)} %param.15) | copy-start | bytes 3145732
  11.5 2.7 copy-start.8
  11.5 4.3 copy-start.10
  11.5 4.4 copy-start.11
  14.1 117.2 %all-gather.5.cloned.1.call-start = ((), (), s32[]{:S(2)}) async-start(), calls=%async_computation.2 | async-start | bytes 2359296 | tf_op jit(solution)/shard_map/all_gather | solution.py:46
  14.9 191.8 %all-gather.7.cloned.1.call-start = ((), (), s32[]{:S(2)}) async-start(), calls=%async_computation.4 | async-start | bytes 4718592 | tf_op jit(solution)/shard_map/all_gather | solution.py:35
  15.8 304.9 %reduce-scatter.5.cloned.1.call-start = ((), (), s32[]{:S(2)}) async-start(), calls=%async_computation.6 | async-start | bytes 589824 | tf_op jit(solution)/shard_map/reduce_scatter | solution.py:52
  131.3 6.6 %copy-start.5 = (f32[1,256,512]{2,1,0:T(8,128)S(1)}, f32[1,256,512]{2,1,0:T(8,128)}, u32[]{:S(2)}) copy-start(f32[1,256,512]{2,1,0:T(8,128)} %param.21) | copy-start | bytes 1572868
  134.5 72.2 %copy-start.12 = (s32[1,8]{1,0:T(1,128)S(1)}, s32[1,8]{1,0:T(1,128)}, u32[]{:S(2)}) copy-start(s32[1,8]{1,0:T(1,128)} %param.17) | copy-start | bytes 100
  253.7 3.5 copy-start.1
  257.2 1.0 copy-start.4
  257.2 1.4 copy-start.6
  257.2 4.0 copy-start.3
  258.6 1.5 copy-start.9
  260.0 115.4 %all-gather.9.cloned.1.call-start = ((), (), s32[]{:S(2)}) async-start(), calls=%async_computation.5 | async-start | bytes 2359296 | tf_op jit(solution)/shard_map/all_gather | solution.py:46
  260.6 188.6 %all-gather.11.cloned.1.call-start = ((), (), s32[]{:S(2)}) async-start(), calls=%async_computation.7 | async-start | bytes 4718592 | tf_op jit(solution)/shard_map/all_gather | solution.py:35
  378.4 6.6 %copy-start.7 = (f32[1,256,512]{2,1,0:T(8,128)S(1)}, f32[1,256,512]{2,1,0:T(8,128)}, u32[]{:S(2)}) copy-start(f32[1,256,512]{2,1,0:T(8,128)} %param.21) | copy-start | bytes 1572868
Sparse Core Ops, SparseCore 0:
  14.2 63.9 reduce-scatter.2
  80.4 50.8 all-gather.4
  134.0 72.6 all-gather.6
  260.1 60.5 reduce-scatter.4
  322.6 52.8 all-gather.8
  377.5 71.6 all-gather.10
where the time goes:
time: 515 us; the launch traced here: 514 us
  waiting for transfers between devices  276 us (54%)
  blocking collectives  77.6 us (15%)
  matrix products  65.5 us (13%)
  loops' own time  43.2 us (8%)
  local copies, waits for them, and re-layouts  34.8 us (7%)
  between operations  15.2 us (3%)
    all_gather x2, waiting for transfers between devices, multiply(): lax.all_gather(packed, 'col', axis=0, tiled=True)  132 us
    reduce_scatter x2, waiting for transfers between devices, multiply(): portion = lax.psum_scatter(upward, 'col', scatter_dimension=1, tiled=True)  118 us
    all_gather x2, blocking collectives, multiply(): far_parent = lax.all_gather(far_portion, 'col', axis=1, tiled=True)  65.6 us
    another operation x2, loops' own time, multiply(): near_sum = lax.fori_loop(0, near_count[0], add_slot, empty)  43.2 us
    dot_general x16, matrix products, add_slot(): jnp.dot(near_block, source, preferred_element_type=jnp.float32)  38.6 us
    all_gather x2, waiting for transfers between devices, multiply(): lax.all_gather(skeleton, 'col', axis=0, tiled=True)  25 us
    all_gather x2, blocking collectives, multiply(): lax.all_gather(portion, 'row', axis=0, tiled=True)  11.9 us
  transfers between devices with their start and end apart: 6, of which 6 were waited for; matrix products, arithmetic and copies ran while one was open for 5% of the time, Pallas kernels for 0%

commit v1 on v0

--- a/solution.py
+++ b/solution.py
@@ -56,7 +56,14 @@
         far_portion = jnp.einsum(
             "kab,kbp->ap", parent_link_blocks[0], every_parent[parent_links[0]], precision=highest
         )
-        far_parent = lax.all_gather(far_portion, "col", axis=1, tiled=True)
+        ring = [far_portion]
+        for hop in range(7):
+            ring.append(lax.ppermute(ring[-1], "col", [(dev, (dev + 1) % 8) for dev in range(8)]))
+        far_parent = jnp.roll(
+            jnp.concatenate(ring[::-1], axis=1),
+            (lax.axis_index("col") + 1) * ring[0].shape[1],
+            axis=1,
+        )
         combined = (coupled + jnp.dot(transfer, far_parent, precision=highest)) * rank_mask
         return jnp.dot(leaf_basis, combined, precision=highest) + near_sum
 

time: 515 us -> 520 us (level)
  blocking collectives: 77.6 us -> 11.9 us
  waiting for transfers between devices: 276 us -> 336 us
  local copies, waits for them, and re-layouts: 34.8 us -> 41.7 us
    ppermute x0 -> x14, waiting for transfers between devices: none -> 105 us  [multiply(): lax.ppermute(ring[-1], 'col', [(dev, (dev + 1) % 8) for dev in range(8)])]
    all_gather x2 -> x0, blocking collectives: 65.6 us -> none  [multiply(): far_parent = lax.all_gather(far_portion, 'col', axis=1, tiled=True)]
    all_gather x2, waiting for transfers between devices: 25 us -> 0.02 us  [multiply(): lax.all_gather(skeleton, 'col', axis=0, tiled=True)]
    all_gather x2, waiting for transfers between devices: 132 us -> 107 us  [multiply(): lax.all_gather(packed, 'col', axis=0, tiled=True)]
    unnamed x29 -> x43, local copies, waits for them, and re-layouts: 5.65 us -> 11.7 us
  transfers between devices with their start and end apart: 6 -> 20, of which waited for: 6 -> 18; matrix products, arithmetic and copies ran while one was open for 5% -> 7% of each run, Pallas kernels for 0% -> 0%
where the time goes in v1:
time: 520 us; the launch traced here: 519 us
  waiting for transfers between devices  336 us (65%)
  matrix products  66.6 us (13%)
  loops' own time  43.4 us (8%)
  local copies, waits for them, and re-layouts  41.7 us (8%)
  between operations  15.3 us (3%)
  blocking collectives  11.9 us (2%)
    reduce_scatter x2, waiting for transfers between devices, multiply(): portion = lax.psum_scatter(upward, 'col', scatter_dimension=1, tiled=True)  122 us
    all_gather x2, waiting for transfers between devices, multiply(): lax.all_gather(packed, 'col', axis=0, tiled=True)  107 us
    ppermute x14, waiting for transfers between devices, multiply(): lax.ppermute(ring[-1], 'col', [(dev, (dev + 1) % 8) for dev in range(8)])  105 us
    another operation x2, loops' own time, multiply(): near_sum = lax.fori_loop(0, near_count[0], add_slot, empty)  43.4 us
    dot_general x16, matrix products, add_slot(): jnp.dot(near_block, source, preferred_element_type=jnp.float32)  38.6 us
    all_gather x2, blocking collectives, multiply(): lax.all_gather(portion, 'row', axis=0, tiled=True)  11.9 us
    unnamed x43, local copies, waits for them, and re-layouts  11.7 us
  transfers between devices with their start and end apart: 20, of which 18 were waited for; matrix products, arithmetic and copies ran while one was open for 7% of the time, Pallas kernels for 0%

profile of v1, /device:TPU:4, one launch (start us, length us, event | category | flops | bytes accessed | tf_op | source)
XLA Modules:
  0.0 518.6 jit_solution(10481920622310867863)
XLA Ops:
  8.0 3.5 convolution_multiply_fusion.1
  11.5 2.6 convolution_bitcast_fusion.3
  15.9 62.3 %reduce-scatter.3.cloned.1.call-done = f32[512,32]{0,1:T(8,128)} async-done(((f32[512,256]{0,1:T(8,128)}), f32[512,32]{0,1:T(8,128)}) %reduce-scatter.3.cloned.1.call-update) | async-done | bytes 65552 | tf_op jit(solution)/shard_map/reduce_scatter | solution.py:52
  78.2 6.0 %all_gather.19 = f32[2048,32]{0,1:T(8,128)S(1)} all-gather(f32[512,32]{0,1:T(8,128)} %reduce-scatter.3.cloned.1.call-done), channel_id=1, replica_groups=mesh['row'=4,'col'=8] {'row'}, dimensions={0}, use_global_device_ids=true | all-gather | bytes 327680 | tf_op jit(solution)/shard_map/all_gather | solution.py:53
  88.2 7.1 %collective-permute-done = f32[512,32]{0,1:T(8,128)S(1)} collective-permute-done((f32[512,32]{0,1:T(8,128)S(1)}, f32[512,32]{0,1:T(8,128)S(1)}, u32[]{:S(2)}, u32[]{:S(2)}) %collective-permute-start) | collective-permute-done | bytes 65568 | tf_op jit(solution)/shard_map/ppermute | solution.py:61
  95.3 8.1 %collective-permute-done.1 = f32[512,32]{0,1:T(8,128)S(1)} collective-permute-done((f32[512,32]{0,1:T(8,128)S(1)}, f32[512,32]{0,1:T(8,128)S(1)}, u32[]{:S(2)}, u32[]{:S(2)}) %collective-permute-start.1) | collective-permute-done | bytes 65568 | tf_op jit(solution)/shard_map/ppermute | solution.py:61
  103.4 7.0 %collective-permute-done.2 = f32[512,32]{0,1:T(8,128)S(1)} collective-permute-done((f32[512,32]{0,1:T(8,128)S(1)}, f32[512,32]{0,1:T(8,128)S(1)}, u32[]{:S(2)}, u32[]{:S(2)}) %collective-permute-start.2) | collective-permute-done | bytes 65568 | tf_op jit(solution)/shard_map/ppermute | solution.py:61
  110.3 8.7 %collective-permute-done.3 = f32[512,32]{0,1:T(8,128)S(1)} collective-permute-done((f32[512,32]{0,1:T(8,128)S(1)}, f32[512,32]{0,1:T(8,128)S(1)}, u32[]{:S(2)}, u32[]{:S(2)}) %collective-permute-start.3) | collective-permute-done | bytes 65568 | tf_op jit(solution)/shard_map/ppermute | solution.py:61
  119.0 8.0 %collective-permute-done.4 = f32[512,32]{0,1:T(8,128)S(1)} collective-permute-done((f32[512,32]{0,1:T(8,128)S(1)}, f32[512,32]{0,1:T(8,128)S(1)}, u32[]{:S(2)}, u32[]{:S(2)}) %collective-permute-start.4) | collective-permute-done | bytes 65568 | tf_op jit(solution)/shard_map/ppermute | solution.py:61
  127.1 8.2 %collective-permute-done.5 = f32[512,32]{0,1:T(8,128)S(1)} collective-permute-done((f32[512,32]{0,1:T(8,128)S(1)}, f32[512,32]{0,1:T(8,128)S(1)}, u32[]{:S(2)}, u32[]{:S(2)}) %collective-permute-start.5) | collective-permute-done | bytes 65568 | tf_op jit(solution)/shard_map/ppermute | solution.py:61
  135.3 7.0 %collective-permute-done.6 = f32[512,32]{0,1:T(8,128)S(1)} collective-permute-done((f32[512,32]{0,1:T(8,128)S(1)}, f32[512,32]{0,1:T(8,128)S(1)}, u32[]{:S(2)}, u32[]{:S(2)}) %collective-permute-start.6) | collective-permute-done | bytes 65568 | tf_op jit(solution)/shard_map/ppermute | solution.py:61
  142.4 3.4 gather_fusion
  145.8 3.4 convolution_bitcast_fusion.5
  149.8 59.0 %all-gather.7.cloned.1.call-done = bf16[8192,256]{1,0:T(8,128)(2,1)} async-done(((bf16[1024,256]{1,0:T(8,128)(2,1)}), bf16[8192,256]{1,0:T(8,128)(2,1)}) %all-gather.7.cloned.1.call-update) | async-done | bytes 4194320 | tf_op jit(solution)/shard_map/all_gather | solution.py:35
  208.9 45.8 %while.20 = (s32[]{:T(128)}, f32[1024,256]{1,0:T(8,128)S(1)}, s32[]{:T(128)}, bf16[8,1024,1024]{2,1,0:T(8,128)(2,1)}, s32[8]{0:T(128)S(1)}, /*index=5*/bf16[8,10...) while((s32[]{:T(128)}, f32[1024,256]{1,0:T(8,128)S(1)}, s32[]{:T(128)}, ...), condition=%wide.region_2.4_spmd, body=%wide.region_1.3_spmd.sunk | while | flops 537133056 | bytes 4718773 | solution.py:44
  212.1 2.4 fusion.73
  217.7 2.4 fusion.73
  223.3 2.4 fusion.73
  229.0 2.4 fusion.73
  234.6 2.4 fusion.73
  240.2 2.4 fusion.73
  245.8 2.4 fusion.73
  251.4 2.4 fusion.73
  256.0 3.5 fusion.50
  263.5 59.5 %reduce-scatter.5.cloned.1.call-done = f32[512,32]{0,1:T(8,128)} async-done(((f32[512,256]{0,1:T(8,128)}), f32[512,32]{0,1:T(8,128)}) %reduce-scatter.5.cloned.1.call-update) | async-done | bytes 65552 | tf_op jit(solution)/shard_map/reduce_scatter | solution.py:52
  323.0 6.0 %all_gather.22 = f32[2048,32]{0,1:T(8,128)S(1)} all-gather(f32[512,32]{0,1:T(8,128)} %reduce-scatter.5.cloned.1.call-done), channel_id=1, replica_groups=mesh['row'=4,'col'=8] {'row'}, dimensions={0}, use_global_device_ids=true | all-gather | bytes 327680 | tf_op jit(solution)/shard_map/all_gather | solution.py:53
  332.9 7.4 %collective-permute-done.7 = f32[512,32]{0,1:T(8,128)S(1)} collective-permute-done((f32[512,32]{0,1:T(8,128)S(1)}, f32[512,32]{0,1:T(8,128)S(1)}, u32[]{:S(2)}, u32[]{:S(2)}) %collective-permute-start.7) | collective-permute-done | bytes 65568 | tf_op jit(solution)/shard_map/ppermute | solution.py:61
  340.3 7.0 %collective-permute-done.8 = f32[512,32]{0,1:T(8,128)S(1)} collective-permute-done((f32[512,32]{0,1:T(8,128)S(1)}, f32[512,32]{0,1:T(8,128)S(1)}, u32[]{:S(2)}, u32[]{:S(2)}) %collective-permute-start.8) | collective-permute-done | bytes 65568 | tf_op jit(solution)/shard_map/ppermute | solution.py:61
  347.3 7.0 %collective-permute-done.9 = f32[512,32]{0,1:T(8,128)S(1)} collective-permute-done((f32[512,32]{0,1:T(8,128)S(1)}, f32[512,32]{0,1:T(8,128)S(1)}, u32[]{:S(2)}, u32[]{:S(2)}) %collective-permute-start.9) | collective-permute-done | bytes 65568 | tf_op jit(solution)/shard_map/ppermute | solution.py:61
  354.3 8.3 %collective-permute-done.10 = f32[512,32]{0,1:T(8,128)S(1)} collective-permute-done((f32[512,32]{0,1:T(8,128)S(1)}, f32[512,32]{0,1:T(8,128)S(1)}, u32[]{:S(2)}, u32[]{:S(2)}) %collective-permute-start.10) | collective-permute-done | bytes 65568 | tf_op jit(solution)/shard_map/ppermute | solution.py:61
  362.6 8.7 %collective-permute-done.11 = f32[512,32]{0,1:T(8,128)S(1)} collective-permute-done((f32[512,32]{0,1:T(8,128)S(1)}, f32[512,32]{0,1:T(8,128)S(1)}, u32[]{:S(2)}, u32[]{:S(2)}) %collective-permute-start.11) | collective-permute-done | bytes 65568 | tf_op jit(solution)/shard_map/ppermute | solution.py:61
  371.4 8.9 %collective-permute-done.12 = f32[512,32]{0,1:T(8,128)} collective-permute-done((f32[512,32]{0,1:T(8,128)S(1)}, f32[512,32]{0,1:T(8,128)}, u32[]{:S(2)}, u32[]{:S(2)}) %collective-permute-start.12) | collective-permute-done | bytes 65568 | tf_op jit(solution)/shard_map/ppermute | solution.py:61
  381.6 2.5 copy.26
  384.1 3.4 collective-permute-done.13
  394.3 3.0 copy.28
  397.3 3.2 gather_fusion.2
  400.5 3.4 convolution_bitcast_fusion.4
  405.6 48.4 %all-gather.11.cloned.1.call-done = bf16[8192,256]{0,1:T(8,128)(2,1)} async-done(((bf16[1024,256]{0,1:T(8,128)(2,1)}), bf16[8192,256]{0,1:T(8,128)(2,1)}) %all-gather.11.cloned.1.call-update) | async-done | bytes 4194320 | tf_op jit(solution)/shard_map/all_gather | solution.py:35
  454.0 6.4 %copy.29 = bf16[8192,256]{1,0:T(8,128)(2,1)} copy(bf16[8192,256]{0,1:T(8,128)(2,1)} %all-gather.11.cloned.1.call-done) | data formatting | bytes 8388608 | tf_op jit(solution)/shard_map/while | solution.py:44
  460.5 45.6 %while.21 = (s32[]{:T(128)}, f32[1024,256]{1,0:T(8,128)S(1)}, s32[]{:T(128)}, bf16[8,1024,1024]{2,1,0:T(8,128)(2,1)}, s32[8]{0:T(128)S(1)}, /*index=5*/bf16[8,10...) while((s32[]{:T(128)}, f32[1024,256]{1,0:T(8,128)S(1)}, s32[]{:T(128)}, ...), condition=%wide.region_5.7_spmd, body=%wide.region_4.6_spmd.sunk | while | flops 537133056 | bytes 4718773 | solution.py:44
  463.7 2.4 fusion.76
  469.3 2.4 fusion.76
  475.0 2.4 fusion.76
  480.6 2.4 fusion.76
  486.2 2.4 fusion.76
  491.8 2.4 fusion.76
  497.5 2.4 fusion.76
  507.5 2.9 fusion.25
  (109 shorter events, 40.1 us)
Async XLA Ops:
  7.2 77.6 %copy-start = (f32[1,2,512,512]{3,2,1,0:T(8,128)S(1)}, f32[1,2,512,512]{3,2,1,0:T(8,128)}, u32[]{:S(2)}) copy-start(f32[1,2,512,512]{3,2,1,0:T(8,128)} %param.27) | copy-start | bytes 6291460
  7.2 71.0 %reduce-scatter.3.cloned.1.call-start = ((), (), s32[]{:S(2)}) async-start(), calls=%async_computation.3 | async-start | bytes 589824 | tf_op jit(solution)/shard_map/reduce_scatter | solution.py:52
  8.0 6.9 %copy-start.2 = (f32[1024,256]{1,0:T(8,128)S(1)}, f32[1024,256]{1,0:T(8,128)}, u32[]{:S(2)}) copy-start(f32[1024,256]{1,0:T(8,128)} %param.17) | copy-start | bytes 3145732
  11.5 2.7 copy-start.8
  11.5 4.3 copy-start.10
  14.1 128.3 %all-gather.5.cloned.1.call-start = ((), (), s32[]{:S(2)}) async-start(), calls=%async_computation.2 | async-start | bytes 2359296 | tf_op jit(solution)/shard_map/all_gather | solution.py:46
  14.9 194.0 %all-gather.7.cloned.1.call-start = ((), (), s32[]{:S(2)}) async-start(), calls=%async_computation.4 | async-start | bytes 4718592 | tf_op jit(solution)/shard_map/all_gather | solution.py:35
  15.8 307.2 %reduce-scatter.5.cloned.1.call-start = ((), (), s32[]{:S(2)}) async-start(), calls=%async_computation.6 | async-start | bytes 589824 | tf_op jit(solution)/shard_map/reduce_scatter | solution.py:52
  15.9 111.2 %copy-start.11 = (s32[1,4]{1,0:T(1,128)S(1)}, s32[1,4]{1,0:T(1,128)}, u32[]{:S(2)}) copy-start(s32[1,4]{1,0:T(1,128)} %param.24) | copy-start | bytes 52
  86.8 8.5 %collective-permute-start = (f32[512,32]{0,1:T(8,128)S(1)}, f32[512,32]{0,1:T(8,128)S(1)}, u32[]{:S(2)}, u32[]{:S(2)}) collective-permute-start(f32[512,32]{0,1:T(8,128)S(1)} %fusion.28), channel_id=1, source_target_pairs={{0,1},{1,2},{2,3},{3,4},{4,5},{5,6},{6,7},{7,0},{8,9},{9,10},{10,1... | collective-permute-start | bytes 196616 | tf_op jit(solution)/shard_map/ppermute | solution.py:61
  95.3 8.1 %collective-permute-start.1 = (f32[512,32]{0,1:T(8,128)S(1)}, f32[512,32]{0,1:T(8,128)S(1)}, u32[]{:S(2)}, u32[]{:S(2)}) collective-permute-start(f32[512,32]{0,1:T(8,128)S(1)} %collective-permute-done), channel_id=1, source_target_pairs={{0,1},{1,2},{2,3},{3,4},{4,5},{5,6},{6,7},{7,0},{8,9},{9,10},{10,1... | collective-permute-start | bytes 196616 | tf_op jit(solution)/shard_map/ppermute | solution.py:61
  103.4 7.0 %collective-permute-start.2 = (f32[512,32]{0,1:T(8,128)S(1)}, f32[512,32]{0,1:T(8,128)S(1)}, u32[]{:S(2)}, u32[]{:S(2)}) collective-permute-start(f32[512,32]{0,1:T(8,128)S(1)} %collective-permute-done.1), channel_id=1, source_target_pairs={{0,1},{1,2},{2,3},{3,4},{4,5},{5,6},{6,7},{7,0},{8,9},{9,10},{10,1... | collective-permute-start | bytes 196616 | tf_op jit(solution)/shard_map/ppermute | solution.py:61
  110.3 8.7 %collective-permute-start.3 = (f32[512,32]{0,1:T(8,128)S(1)}, f32[512,32]{0,1:T(8,128)S(1)}, u32[]{:S(2)}, u32[]{:S(2)}) collective-permute-start(f32[512,32]{0,1:T(8,128)S(1)} %collective-permute-done.2), channel_id=1, source_target_pairs={{0,1},{1,2},{2,3},{3,4},{4,5},{5,6},{6,7},{7,0},{8,9},{9,10},{10,1... | collective-permute-start | bytes 196616 | tf_op jit(solution)/shard_map/ppermute | solution.py:61
  119.0 8.0 %collective-permute-start.4 = (f32[512,32]{0,1:T(8,128)S(1)}, f32[512,32]{0,1:T(8,128)S(1)}, u32[]{:S(2)}, u32[]{:S(2)}) collective-permute-start(f32[512,32]{0,1:T(8,128)S(1)} %collective-permute-done.3), channel_id=1, source_target_pairs={{0,1},{1,2},{2,3},{3,4},{4,5},{5,6},{6,7},{7,0},{8,9},{9,10},{10,1... | collective-permute-start | bytes 196616 | tf_op jit(solution)/shard_map/ppermute | solution.py:61
  127.0 8.2 %collective-permute-start.5 = (f32[512,32]{0,1:T(8,128)S(1)}, f32[512,32]{0,1:T(8,128)S(1)}, u32[]{:S(2)}, u32[]{:S(2)}) collective-permute-start(f32[512,32]{0,1:T(8,128)S(1)} %collective-permute-done.4), channel_id=1, source_target_pairs={{0,1},{1,2},{2,3},{3,4},{4,5},{5,6},{6,7},{7,0},{8,9},{9,10},{10,1... | collective-permute-start | bytes 196616 | tf_op jit(solution)/shard_map/ppermute | solution.py:61
  135.3 7.0 %collective-permute-start.6 = (f32[512,32]{0,1:T(8,128)S(1)}, f32[512,32]{0,1:T(8,128)S(1)}, u32[]{:S(2)}, u32[]{:S(2)}) collective-permute-start(f32[512,32]{0,1:T(8,128)S(1)} %collective-permute-done.5), channel_id=1, source_target_pairs={{0,1},{1,2},{2,3},{3,4},{4,5},{5,6},{6,7},{7,0},{8,9},{9,10},{10,1... | collective-permute-start | bytes 196616 | tf_op jit(solution)/shard_map/ppermute | solution.py:61
  142.4 6.8 %copy-start.5 = (f32[1,256,512]{2,1,0:T(8,128)S(1)}, f32[1,256,512]{2,1,0:T(8,128)}, u32[]{:S(2)}) copy-start(f32[1,256,512]{2,1,0:T(8,128)} %param.23) | copy-start | bytes 1572868
  145.8 63.1 %copy-start.12 = (s32[1,8]{1,0:T(1,128)S(1)}, s32[1,8]{1,0:T(1,128)}, u32[]{:S(2)}) copy-start(s32[1,8]{1,0:T(1,128)} %param.19) | copy-start | bytes 100
  256.0 3.5 copy-start.1
  259.5 1.0 copy-start.4
  259.5 1.4 copy-start.6
  260.9 1.5 copy-start.9
  262.3 132.0 %all-gather.9.cloned.1.call-start = ((), (), s32[]{:S(2)}) async-start(), calls=%async_computation.5 | async-start | bytes 2359296 | tf_op jit(solution)/shard_map/all_gather | solution.py:46
  262.9 191.1 %all-gather.11.cloned.1.call-start = ((), (), s32[]{:S(2)}) async-start(), calls=%async_computation.7 | async-start | bytes 4718592 | tf_op jit(solution)/shard_map/all_gather | solution.py:35
  263.5 116.8 %copy-start.3 = (f32[1024,256]{1,0:T(8,128)S(1)}, f32[1024,256]{1,0:T(8,128)}, u32[]{:S(2)}) copy-start(f32[1024,256]{1,0:T(8,128)} %param.17) | copy-start | bytes 3145732
  331.6 8.7 %collective-permute-start.7 = (f32[512,32]{0,1:T(8,128)S(1)}, f32[512,32]{0,1:T(8,128)S(1)}, u32[]{:S(2)}, u32[]{:S(2)}) collective-permute-start(f32[512,32]{0,1:T(8,128)S(1)} %fusion.31), channel_id=1, source_target_pairs={{0,1},{1,2},{2,3},{3,4},{4,5},{5,6},{6,7},{7,0},{8,9},{9,10},{10,1... | collective-permute-start | bytes 196616 | tf_op jit(solution)/shard_map/ppermute | solution.py:61
  340.3 7.0 %collective-permute-start.8 = (f32[512,32]{0,1:T(8,128)S(1)}, f32[512,32]{0,1:T(8,128)S(1)}, u32[]{:S(2)}, u32[]{:S(2)}) collective-permute-start(f32[512,32]{0,1:T(8,128)S(1)} %collective-permute-done.7), channel_id=1, source_target_pairs={{0,1},{1,2},{2,3},{3,4},{4,5},{5,6},{6,7},{7,0},{8,9},{9,10},{10,1... | collective-permute-start | bytes 196616 | tf_op jit(solution)/shard_map/ppermute | solution.py:61
  347.3 7.0 %collective-permute-start.9 = (f32[512,32]{0,1:T(8,128)S(1)}, f32[512,32]{0,1:T(8,128)S(1)}, u32[]{:S(2)}, u32[]{:S(2)}) collective-permute-start(f32[512,32]{0,1:T(8,128)S(1)} %collective-permute-done.8), channel_id=1, source_target_pairs={{0,1},{1,2},{2,3},{3,4},{4,5},{5,6},{6,7},{7,0},{8,9},{9,10},{10,1... | collective-permute-start | bytes 196616 | tf_op jit(solution)/shard_map/ppermute | solution.py:61
  354.3 8.3 %collective-permute-start.10 = (f32[512,32]{0,1:T(8,128)S(1)}, f32[512,32]{0,1:T(8,128)S(1)}, u32[]{:S(2)}, u32[]{:S(2)}) collective-permute-start(f32[512,32]{0,1:T(8,128)S(1)} %collective-permute-done.9), channel_id=1, source_target_pairs={{0,1},{1,2},{2,3},{3,4},{4,5},{5,6},{6,7},{7,0},{8,9},{9,10},{10,1... | collective-permute-start | bytes 196616 | tf_op jit(solution)/shard_map/ppermute | solution.py:61
  362.6 8.7 %collective-permute-start.11 = (f32[512,32]{0,1:T(8,128)S(1)}, f32[512,32]{0,1:T(8,128)S(1)}, u32[]{:S(2)}, u32[]{:S(2)}) collective-permute-start(f32[512,32]{0,1:T(8,128)S(1)} %collective-permute-done.10), channel_id=1, source_target_pairs={{0,1},{1,2},{2,3},{3,4},{4,5},{5,6},{6,7},{7,0},{8,9},{9,10},{10,1... | collective-permute-start | bytes 196616 | tf_op jit(solution)/shard_map/ppermute | solution.py:61
  371.4 8.9 %collective-permute-start.12 = (f32[512,32]{0,1:T(8,128)S(1)}, f32[512,32]{0,1:T(8,128)}, u32[]{:S(2)}, u32[]{:S(2)}) collective-permute-start(f32[512,32]{0,1:T(8,128)S(1)} %collective-permute-done.11), channel_id=1, source_target_pairs={{0,1},{1,2},{2,3},{3,4},{4,5},{5,6},{6,7},{7,0},{8,9},{9,10},{10,1... | collective-permute-start | bytes 196616 | tf_op jit(solution)/shard_map/ppermute | solution.py:61
  380.3 7.3 %collective-permute-start.13 = (f32[512,32]{0,1:T(8,128)}, f32[512,32]{0,1:T(8,128)}, u32[]{:S(2)}, u32[]{:S(2)}) collective-permute-start(f32[512,32]{0,1:T(8,128)} %collective-permute-done.12), channel_id=1, source_target_pairs={{0,1},{1,2},{2,3},{3,4},{4,5},{5,6},{6,7},{7,0},{8,9},{9,10},{10,1... | collective-permute-start | bytes 196616 | tf_op jit(solution)/shard_map/ppermute | solution.py:61
  397.3 6.6 %copy-start.7 = (f32[1,256,512]{2,1,0:T(8,128)S(1)}, f32[1,256,512]{2,1,0:T(8,128)}, u32[]{:S(2)}) copy-start(f32[1,256,512]{2,1,0:T(8,128)} %param.23) | copy-start | bytes 1572868
Sparse Core Ops, SparseCore 0:
  14.2 63.9 reduce-scatter.2
  80.3 52.4 all-gather.4
  135.6 73.1 all-gather.6
  262.4 60.5 reduce-scatter.4
  324.9 54.2 all-gather.8
  381.3 72.7 all-gather.10
